TPU v7x, 128 devices: a whole 4x4x4 slice. The times are simulated.
128 devices in a mesh: occ: 4 (over x), vir: 32 (over y, z, core).
Axes of the slice: x: 4, y: 4, z: 4, core: 2. Of those that a mesh axis runs over, the one named last changes fastest.
Arguments:
- amplitudes: bfloat16 [256, 262144], P('occ', 'vir'), may hold values from -6 to 6
- cycle_integrals: bfloat16 [16, 64, 16, 64], P(None, None, 'occ'), may hold values from -0.1875 to 0.1875
- ladder_tiles: bfloat16 [2048, 4, 128, 128], P('vir'), may hold values from -0.25 to 0.25
- ladder_rows: int32 [2048, 4], P('vir'), may hold values from 0 to 2047, as said below
- ladder_count: int32 [2048], P('vir'), may hold values from 2 to 4
- row_gap: float32 [256], P('occ'), may hold values from 1 to 3
- column_energy: float32 [262144], P('vir'), may hold values from 0.5 to 8
Outputs:
- updated: bfloat16 [256, 262144], P('occ', 'vir')
Inputs may be any that keep to these rules, and one draw needn't show every extreme that they name: `ladder_rows`: each entry of column tile c's list names a virtual-pair tile within 2 tiles of c; entry 0 is max(c - 2, 0) and entry 1 is min(c + 2, 2047).
All inputs are finite; a program needn't handle non-finite values.
Results may differ from a plain program's by a relative error of at most 0.0019.
Values may be sent and summed in bfloat16 or wider, within the bound.
A program may use at most 192 MiB of HBM per device.

v0:
```python
import jax
import jax.numpy as jnp
from jax import lax
from jax.sharding import PartitionSpec as P

TILE = 128
NJ = 16
NA = 4096
NB_DEV = 2
KMAX = 4
HT = 2


def extended(block, sides, width):
    for axis, dim in sides:
        count = lax.axis_size(axis)
        forward = [(i, i + 1) for i in range(count - 1)]
        backward = [(target, source) for source, target in forward]
        low = lax.ppermute(
            lax.slice_in_dim(block, block.shape[dim] - width, None, axis=dim), axis, forward
        )
        high = lax.ppermute(lax.slice_in_dim(block, 0, width, axis=dim), axis, backward)
        block = jnp.concatenate([low, block, high], axis=dim)
    return block


def local(
    amplitudes, cycle_integrals, ladder_tiles, ladder_rows, ladder_count, row_gap, column_energy
):
    rows_dev = amplitudes.shape[0]
    cols_dev = amplitudes.shape[1]
    outer_occ = rows_dev // NJ
    four_dim = amplitudes.reshape(outer_occ, NJ, NB_DEV, NA)
    cycle_input = lax.all_to_all(four_dim, "vir", split_axis=3, concat_axis=2, tiled=True)
    tiles_dev = cols_dev // TILE
    padded = extended(amplitudes, (("vir", 1),), HT * TILE)
    own_tiles = lax.axis_index("vir") * tiles_dev + jnp.arange(tiles_dev, dtype=jnp.int32)
    relative = ladder_rows - own_tiles[:, None]
    live_mask = jnp.arange(KMAX, dtype=jnp.int32)[None, :] < ladder_count[:, None]
    ladder = jnp.zeros((rows_dev, tiles_dev, TILE), jnp.float32)
    for offset in range(2 * HT + 1):
        window = padded[:, offset * TILE : offset * TILE + cols_dev].reshape(
            rows_dev, tiles_dev, TILE
        )
        for entry in range(KMAX):
            selected = live_mask[:, entry] & (relative[:, entry] == offset - HT)
            masked = jnp.where(
                selected[:, None, None], ladder_tiles[:, entry], jnp.zeros((), jnp.bfloat16)
            )
            ladder = ladder + jnp.einsum(
                "rcp,cpq->rcq", window, masked, preferred_element_type=jnp.float32
            )
    ladder = ladder.reshape(rows_dev, cols_dev)
    all_rows = lax.all_gather(cycle_input, "occ", axis=0, tiled=True)
    cycle_part = jnp.einsum(
        "ijba,jbkc->ikca", all_rows, cycle_integrals, preferred_element_type=jnp.float32
    ).astype(jnp.bfloat16)
    cycle_pair = lax.all_to_all(
        lax.all_to_all(cycle_part, "occ", split_axis=0, concat_axis=1, tiled=True),
        "vir",
        split_axis=2,
        concat_axis=3,
        tiled=True,
    )
    cycle_flat = cycle_pair.reshape(rows_dev, cols_dev)
    denominator = row_gap[:, None] + column_energy[None, :]
    updated = (
        amplitudes.astype(jnp.float32) + (cycle_flat.astype(jnp.float32) + ladder) / denominator
    )
    return updated.astype(jnp.bfloat16)


def solution(mesh):
    in_specs = (
        P("occ", "vir"),
        P(None, None, "occ", None),
        P("vir", None, None, None),
        P("vir", None),
        P("vir"),
        P("occ"),
        P("vir"),
    )
    out_specs = P("occ", "vir")
    return jax.shard_map(local, mesh=mesh, in_specs=in_specs, out_specs=out_specs, check_vma=False)
```

profile of v0, /device:TPU:1, one launch (start us, length us, event | category | flops | bytes accessed | tf_op | source)
XLA Modules:
  0.0 195.1 jit_solution(11123908715003614297)
XLA Ops:
  6.5 0.8 fusion.152
  7.3 4.9 %collective-permute-start = (bf16[64,256]{1,0:T(8,128)(2,1)S(1)}, bf16[64,256]{1,0:T(8,128)(2,1)S(1)}, u32[]{:S(2)}, u32[]{:S(2)}) collective-permute-start(bf16[64,256]{1,0:T(8,128)(2,1)S(1)} %get-tuple-element.11), channel_id=1, source_target_pairs={{0,1},{1,2},{2,3},{3,4},{4,5},{5,6},{6,7},{7,8},{8,9},{9,10},{10,1... | collective-permute-start | bytes 98312 | tf_op jit(solution)/shard_map/ppermute | solution.py:19
  12.2 1.9 collective-permute-start.1
  14.2 1.8 reshape.294
  16.0 9.4 %copy.133 = bf16[4,16,2,4096]{1,0,2,3:T(4,128)(2,1)} copy(bf16[4,16,2,4096]{3,2,1,0:T(2,128)(2,1)S(1)} %reshape.294) | data formatting | bytes 2097152 | tf_op jit(solution)/shard_map/reshape | solution.py:33
  25.5 11.2 %reshape.306 = bf16[32,2,8192]{2,1,0:T(2,128)(2,1)} reshape(bf16[4096,2,4,16]{3,2,1,0:T(4,128)(2,1)} %bitcast.213) | data formatting | bytes 2097152
  36.7 8.4 %all-to-all-start = ((bf16[32,2,8192]{2,1,0:T(2,128)(2,1)}), bf16[32,2,8192]{2,1,0:T(2,128)(2,1)S(1)}, u32[]{:S(2)}, u32[]{:S(2)}) async-start(bf16[32,2,8192]{2,1,0:T(2,128)(2,1)} %reshape.306), calls=%async_computation | async-start | bytes 2097152 | tf_op jit(solution)/shard_map/all_to_all | solution.py:34
  45.3 3.7 %fusion.12 = f32[64,128,64]{1,2,0:T(8,128)} fusion(pred[64]{0:T(512)(128)(4,1)S(1)} %get-tuple-element.23, bf16[64,4,128,128]{3,2,1,0:T(8,128)(2,1)} %param.9, bf16[64,8192]{1,0:T(8,128)(2,1)S(1)} %copy-done), kind=kOutput, calls=%fused_computation.23 | convolution fusion | flops 135266304 | bytes 5242944 | tf_op jit(solution)/shard_map/rcp,cpq->rcq/dot_general | solution.py:50
  49.0 3.6 %fusion.17 = f32[64,128,64]{1,2,0:T(8,128)} fusion(pred[64]{0:T(512)(128)(4,1)S(1)} %get-tuple-element.15, bf16[64,4,128,128]{3,2,1,0:T(8,128)(2,1)} %param.9, bf16[64,8192]{1,0:T(8,128)(2,1)S(1)} %copy-done), kind=kOutput, calls=%fused_computation.33 | convolution fusion | flops 135266304 | bytes 5242944 | tf_op jit(solution)/shard_map/rcp,cpq->rcq/dot_general | solution.py:50
  52.7 3.7 %fusion.23 = f32[64,128,64]{1,2,0:T(8,128)} fusion(pred[64]{0:T(512)(128)(4,1)S(1)} %get-tuple-element.19, bf16[64,4,128,128]{3,2,1,0:T(8,128)(2,1)} %param.9, bf16[64,8192]{1,0:T(8,128)(2,1)S(1)} %copy-done), kind=kOutput, calls=%fused_computation.48 | convolution fusion | flops 135266304 | bytes 5242944 | tf_op jit(solution)/shard_map/rcp,cpq->rcq/dot_general | solution.py:50
  56.3 5.7 %all-to-all-done = bf16[32,2,8192]{2,1,0:T(2,128)(2,1)S(1)} async-done(((bf16[32,2,8192]{2,1,0:T(2,128)(2,1)}), bf16[32,2,8192]{2,1,0:T(2,128)(2,1)S(1)}, u32[]{:S(2)}, u32[]{:S(2)}) %all-to-all-start) | async-done | bytes 1048608 | tf_op jit(solution)/shard_map/all_to_all | solution.py:34
  62.0 7.6 %reshape.307 = bf16[4096,2,4,16]{3,2,1,0:T(4,128)(2,1)} reshape(bf16[32,2,8192]{2,1,0:T(2,128)(2,1)S(1)} %all-to-all-done) | data formatting | bytes 2097152
  69.6 12.8 %copy.134 = bf16[4,16,32,2,128]{4,3,2,1,0:T(2,128)(2,1)} copy(bf16[4,16,32,2,128]{1,0,3,4,2:T(4,128)(2,1)} %bitcast.214) | data formatting | bytes 2097152 | tf_op jit(solution)/shard_map/all_to_all | solution.py:34
  82.4 3.9 %fusion.7 = f32[64,128,64]{1,2,0:T(8,128)} fusion(pred[64]{0:T(512)(128)(4,1)S(1)} %get-tuple-element.27, bf16[64,4,128,128]{3,2,1,0:T(8,128)(2,1)} %param.9, bf16[64,8192]{1,0:T(8,128)(2,1)S(1)} %copy-done), kind=kOutput, calls=%fused_computation.13 | convolution fusion | flops 135266304 | bytes 5242944 | tf_op jit(solution)/shard_map/rcp,cpq->rcq/dot_general | solution.py:50
  86.4 0.1 constant_dynamic-update-slice_fusion
  86.5 0.4 slice_bitcast_fusion.1
  86.9 0.3 slice_bitcast_fusion.3
  87.2 2.2 %slice-done.1 = s8[4194304]{0:T(1024)(128)(4,1)S(1)} async-done(((s8[8388608]{0:T(1024)(128)(4,1)}), s8[4194304]{0:T(1024)(128)(4,1)S(1)}, s32[]{:S(2)}) %slice-start.1) | async-done | bytes 4194328
  89.4 2.1 %fusion.13 = f32[64,128,64]{1,2,0:T(8,128)} fusion(pred[64]{0:T(512)(128)(4,1)S(1)} %get-tuple-element.24, bf16[64,4,128,128]{3,2,1,0:T(8,128)(2,1)S(1)} %bitcast.220, bf16[8,64,8,128]{3,2,1,0:T(8,128)(2,1)S(1)} %get-tuple-element.7), kind=kOutput, calls=%fused_computation.24 | convolution fusion | flops 135266304 | bytes 5243392 | tf_op jit(solution)/shard_map/rcp,cpq->rcq/dot_general | solution.py:50
  91.5 2.1 %fusion.18 = f32[64,128,64]{1,2,0:T(8,128)} fusion(pred[64]{0:T(512)(128)(4,1)S(1)} %get-tuple-element.16, bf16[64,4,128,128]{3,2,1,0:T(8,128)(2,1)S(1)} %bitcast.220, bf16[8,64,8,128]{3,2,1,0:T(8,128)(2,1)S(1)} %get-tuple-element.7), kind=kOutput, calls=%fused_computation.34 | convolution fusion | flops 135266304 | bytes 5243392 | tf_op jit(solution)/shard_map/rcp,cpq->rcq/dot_general | solution.py:50
  93.6 2.1 %fusion.14 = f32[64,128,64]{1,2,0:T(8,128)} fusion(pred[64]{0:T(512)(128)(4,1)S(1)} %get-tuple-element.25, bf16[64,4,128,128]{3,2,1,0:T(8,128)(2,1)S(1)} %bitcast.220, bf16[8,64,8,128]{3,2,1,0:T(8,128)(2,1)S(1)} %get-tuple-element.8), kind=kOutput, calls=%fused_computation.25 | convolution fusion | flops 135266304 | bytes 5243392 | tf_op jit(solution)/shard_map/rcp,cpq->rcq/dot_general | solution.py:50
  95.7 2.1 %fusion.19 = f32[64,128,64]{1,2,0:T(8,128)} fusion(pred[64]{0:T(512)(128)(4,1)S(1)} %get-tuple-element.17, bf16[64,4,128,128]{3,2,1,0:T(8,128)(2,1)S(1)} %bitcast.220, bf16[8,64,8,128]{3,2,1,0:T(8,128)(2,1)S(1)} %get-tuple-element.8), kind=kOutput, calls=%fused_computation.35 | convolution fusion | flops 135266304 | bytes 5243392 | tf_op jit(solution)/shard_map/rcp,cpq->rcq/dot_general | solution.py:50
  97.8 2.1 %fusion.24 = f32[64,128,64]{1,2,0:T(8,128)} fusion(pred[64]{0:T(512)(128)(4,1)S(1)} %get-tuple-element.20, bf16[64,4,128,128]{3,2,1,0:T(8,128)(2,1)S(1)} %bitcast.220, bf16[8,64,8,128]{3,2,1,0:T(8,128)(2,1)S(1)} %get-tuple-element.7), kind=kOutput, calls=%fused_computation.49 | convolution fusion | flops 135266304 | bytes 5243392 | tf_op jit(solution)/shard_map/rcp,cpq->rcq/dot_general | solution.py:50
  99.9 2.1 %fusion.8 = f32[64,128,64]{1,2,0:T(8,128)} fusion(pred[64]{0:T(512)(128)(4,1)S(1)} %get-tuple-element.28, bf16[64,4,128,128]{3,2,1,0:T(8,128)(2,1)S(1)} %bitcast.220, bf16[8,64,8,128]{3,2,1,0:T(8,128)(2,1)S(1)} %get-tuple-element.7), kind=kOutput, calls=%fused_computation.14 | convolution fusion | flops 135266304 | bytes 5243392 | tf_op jit(solution)/shard_map/rcp,cpq->rcq/dot_general | solution.py:50
  102.0 2.1 %fusion.9 = f32[64,128,64]{1,2,0:T(8,128)} fusion(pred[64]{0:T(512)(128)(4,1)S(1)} %get-tuple-element.29, bf16[64,4,128,128]{3,2,1,0:T(8,128)(2,1)S(1)} %bitcast.220, bf16[8,64,8,128]{3,2,1,0:T(8,128)(2,1)S(1)} %get-tuple-element.8), kind=kOutput, calls=%fused_computation.15 | convolution fusion | flops 135266304 | bytes 5243392 | tf_op jit(solution)/shard_map/rcp,cpq->rcq/dot_general | solution.py:50
  104.1 2.1 %fusion.11 = f32[64,128,64]{1,2,0:T(8,128)} fusion(pred[64]{0:T(512)(128)(4,1)S(1)} %get-tuple-element.21, bf16[64,4,128,128]{3,2,1,0:T(8,128)(2,1)S(1)} %bitcast.220, bf16[8,64,8,128]{3,2,1,0:T(8,128)(2,1)S(1)} %get-tuple-element.6), kind=kOutput, calls=%fused_computation.22 | convolution fusion | flops 135266304 | bytes 5243392 | tf_op jit(solution)/shard_map/rcp,cpq->rcq/dot_general | solution.py:50
  106.2 2.1 %fusion.16 = f32[64,128,64]{1,2,0:T(8,128)} fusion(pred[64]{0:T(512)(128)(4,1)S(1)} %get-tuple-element.14, bf16[64,4,128,128]{3,2,1,0:T(8,128)(2,1)S(1)} %bitcast.220, bf16[8,64,8,128]{3,2,1,0:T(8,128)(2,1)S(1)} %get-tuple-element.6), kind=kOutput, calls=%fused_computation.32 | convolution fusion | flops 135266304 | bytes 5243392 | tf_op jit(solution)/shard_map/rcp,cpq->rcq/dot_general | solution.py:50
  108.3 2.0 %fusion.22 = f32[64,128,64]{1,2,0:T(8,128)} fusion(pred[64]{0:T(512)(128)(4,1)S(1)} %get-tuple-element.18, bf16[64,4,128,128]{3,2,1,0:T(8,128)(2,1)S(1)} %bitcast.220, bf16[8,64,8,128]{3,2,1,0:T(8,128)(2,1)S(1)} %get-tuple-element.6), kind=kOutput, calls=%fused_computation.47 | convolution fusion | flops 135266304 | bytes 5243392 | tf_op jit(solution)/shard_map/rcp,cpq->rcq/dot_general | solution.py:50
  110.4 2.1 %fusion.21 = f32[64,128,64]{1,2,0:T(8,128)} fusion(pred[64]{0:T(512)(128)(4,1)S(1)} %get-tuple-element.22, bf16[64,4,128,128]{3,2,1,0:T(8,128)(2,1)S(1)} %bitcast.220, bf16[8,64,8,128]{3,2,1,0:T(8,128)(2,1)S(1)} %get-tuple-element.5), kind=kOutput, calls=%fused_computation.46 | convolution fusion | flops 135266304 | bytes 5243392 | tf_op jit(solution)/shard_map/rcp,cpq->rcq/dot_general | solution.py:50
  112.5 2.0 %fusion.5 = f32[64,128,64]{1,2,0:T(8,128)} fusion(pred[64]{0:T(512)(128)(4,1)S(1)} %get-tuple-element.30, bf16[64,4,128,128]{3,2,1,0:T(8,128)(2,1)S(1)} %bitcast.220, bf16[8,64,8,128]{3,2,1,0:T(8,128)(2,1)S(1)} %get-tuple-element.5), kind=kOutput, calls=%fused_computation.11 | convolution fusion | flops 135266304 | bytes 5243392 | tf_op jit(solution)/shard_map/rcp,cpq->rcq/dot_general | solution.py:50
  114.5 13.9 %all-gather.2.cloned.1.call-done = bf16[16,16,64,128]{3,2,1,0:T(8,128)(2,1)} async-done(((bf16[4,16,64,128]{3,2,1,0:T(8,128)(2,1)}), bf16[16,16,64,128]{3,2,1,0:T(8,128)(2,1)}) %all-gather.2.cloned.1.call-update) | async-done | bytes 4194320 | tf_op jit(solution)/shard_map/all_gather | solution.py:54
  128.4 3.5 %fusion.48 = bf16[16,4,64,128]{3,2,0,1:T(8,128)(2,1)S(1)} fusion(bf16[16,16,64,128]{3,2,1,0:T(8,128)(2,1)} %all-gather.2.cloned.1.call-done, bf16[16,64,4,64,1]{3,2,1,0,4:T(4,128)(2,1)S(1)} %bitcast.221), kind=kOutput, calls=%fused_computation.72 | convolution fusion | flops 1074266112 | bytes 5767168 | tf_op jit(solution)/shard_map/ijba,jbkc->ikca/dot_general | solution.py:55
  131.8 1.0 copy.136
  132.9 3.7 %all-to-all-start.1 = ((bf16[16,4,64,128]{3,2,1,0:T(8,128)(2,1)}), bf16[16,4,64,128]{3,2,1,0:T(8,128)(2,1)S(1)}, u32[]{:S(2)}, u32[]{:S(2)}) async-start(bf16[16,4,64,128]{3,2,1,0:T(8,128)(2,1)} %copy.136), calls=%async_computation.1 | async-start | bytes 2097152 | tf_op jit(solution)/shard_map/all_to_all | solution.py:59
  136.6 4.0 %fusion.6 = f32[64,128,64]{1,2,0:T(8,128)} fusion(pred[64]{0:T(512)(128)(4,1)S(1)} %get-tuple-element.26, bf16[64,4,128,128]{3,2,1,0:T(8,128)(2,1)} %param.9, bf16[8,64,8,128]{3,2,1,0:T(8,128)(2,1)} %copy-done.2), kind=kOutput, calls=%fused_computation.12 | convolution fusion | flops 135266304 | bytes 5242944 | tf_op jit(solution)/shard_map/rcp,cpq->rcq/dot_general | solution.py:50
  140.7 3.6 %fusion.10 = f32[64,128,64]{1,2,0:T(8,128)} fusion(pred[64]{0:T(512)(128)(4,1)S(1)} %get-tuple-element.32, bf16[64,4,128,128]{3,2,1,0:T(8,128)(2,1)} %param.9, bf16[8,64,8,128]{3,2,1,0:T(8,128)(2,1)S(1)} %get-tuple-element.5), kind=kOutput, calls=%fused_computation.21 | convolution fusion | flops 135266304 | bytes 5242944 | tf_op jit(solution)/shard_map/rcp,cpq->rcq/dot_general | solution.py:50
  144.3 3.6 %fusion.15 = f32[64,128,64]{1,2,0:T(8,128)} fusion(pred[64]{0:T(512)(128)(4,1)S(1)} %get-tuple-element.31, bf16[64,4,128,128]{3,2,1,0:T(8,128)(2,1)} %param.9, bf16[8,64,8,128]{3,2,1,0:T(8,128)(2,1)S(1)} %get-tuple-element.5), kind=kOutput, calls=%fused_computation.31 | convolution fusion | flops 135266304 | bytes 5242944 | tf_op jit(solution)/shard_map/rcp,cpq->rcq/dot_general | solution.py:50
  147.9 2.9 %all-to-all-done.1 = bf16[16,4,64,128]{3,2,1,0:T(8,128)(2,1)S(1)} async-done(((bf16[16,4,64,128]{3,2,1,0:T(8,128)(2,1)}), bf16[16,4,64,128]{3,2,1,0:T(8,128)(2,1)S(1)}, u32[]{:S(2)}, u32[]{:S(2)}) %all-to-all-start.1) | async-done | bytes 1048608 | tf_op jit(solution)/shard_map/all_to_all | solution.py:59
  150.9 0.1 copy.137
  151.0 1.6 copy.138
  152.6 8.6 %all-to-all-start.2 = ((bf16[4,16,64,128]{3,1,0,2:T(8,128)(2,1)}), bf16[4,16,64,128]{3,1,0,2:T(8,128)(2,1)}, u32[]{:S(2)}, u32[]{:S(2)}) async-start(bf16[4,16,64,128]{3,1,0,2:T(8,128)(2,1)} %copy.138), calls=%async_computation.2 | async-start | bytes 2097152 | tf_op jit(solution)/shard_map/all_to_all | solution.py:58
  161.3 15.6 %fusion.20 = f32[64,8,8,128]{3,2,1,0:T(8,128)S(1)} fusion(f32[64,128,64]{1,2,0:T(8,128)} %fusion.9, f32[64,128,64]{1,2,0:T(8,128)} %fusion.14, f32[64,128,64]{1,2,0:T(8,128)} %fusion.19, f32[64,128,64]{1,2,0:T(8,128)} %fusion.8, f32[64,128,64]{1,2,0:T(8,128)} %fusion.13, f32[64,128,64]{1,2,0:T(8,128)} %fusion.24, f32[64,128,64]{1,2,0:T(8,128)} %fusion.18, ...), kind=kOutput, calls=%fused_computation.38 | convolution fusion | flops 145227776 | bytes 45088832 | tf_op jit(solution)/shard_map/rcp,cpq->rcq/dot_general | solution.py:50
  176.9 1.4 all-to-all-done.2
  178.2 1.4 copy.139
  179.6 0.3 convert_bitcast_fusion
  179.9 2.6 %copy.140 = f32[4,16,2,32,128]{4,3,2,1,0:T(8,128)} copy(f32[4,16,2,32,128]{4,1,2,3,0:T(8,128)S(1)} %convert_bitcast_fusion) | data formatting | bytes 4194304 | tf_op jit(solution)/shard_map/convert_element_type | solution.py:68
  182.5 2.7 %reshape.301 = f32[64,8192]{1,0:T(8,128)} reshape(f32[4,16,2,32,128]{4,3,2,1,0:T(8,128)} %copy.140) | data formatting | bytes 4194304 | tf_op jit(solution)/shard_map/convert_element_type | solution.py:68
  185.2 3.1 %fusion.4 = bf16[64,8192]{1,0:T(8,128)(2,1)} fusion(f32[64,8192]{1,0:T(8,128)} %reshape.301, f32[64,8,8,128]{3,2,1,0:T(8,128)S(1)} %fusion.20, bf16[64,8192]{1,0:T(8,128)(2,1)S(1)} %copy-done, f32[8192]{0:T(1024)S(1)} %copy-done.3, f32[64]{0:T(128)S(1)} %copy-done.5), kind=kLoop, calls=%fused_computation.5 | loop fusion | flops 3145728 | bytes 6324480 | tf_op jit(solution)/shard_map/convert_element_type | solution.py:70
  (32 shorter events, 0.2 us)
Async XLA Ops:
  7.3 79.0 %collective-permute-start = (bf16[64,256]{1,0:T(8,128)(2,1)S(1)}, bf16[64,256]{1,0:T(8,128)(2,1)S(1)}, u32[]{:S(2)}, u32[]{:S(2)}) collective-permute-start(bf16[64,256]{1,0:T(8,128)(2,1)S(1)} %get-tuple-element.11), channel_id=1, source_target_pairs={{0,1},{1,2},{2,3},{3,4},{4,5},{5,6},{6,7},{7,8},{8,9},{9,10},{10,1... | collective-permute-start | bytes 98312 | tf_op jit(solution)/shard_map/ppermute | solution.py:19
  12.2 74.3 %collective-permute-start.1 = (bf16[64,256]{1,0:T(8,128)(2,1)S(1)}, bf16[64,256]{1,0:T(8,128)(2,1)S(1)}, u32[]{:S(2)}, u32[]{:S(2)}) collective-permute-start(bf16[64,256]{1,0:T(8,128)(2,1)S(1)} %get-tuple-element.12), channel_id=1, source_target_pairs={{1,0},{2,1},{3,2},{4,3},{5,4},{6,5},{7,6},{8,7},{9,8},{10,9},{11,1... | collective-permute-start | bytes 98312 | tf_op jit(solution)/shard_map/ppermute | solution.py:22
  36.7 8.5 %copy-start.7 = (s32[64]{0:T(128)S(1)}, s32[64]{0:T(128)}, u32[]{:S(2)}) copy-start(s32[64]{0:T(128)} %param.11) | copy-start | bytes 772
  36.7 8.5 %copy-start.4 = (s32[64,4]{0,1:T(4,128)S(1)}, s32[64,4]{0,1:T(4,128)}, u32[]{:S(2)}) copy-start(s32[64,4]{0,1:T(4,128)} %param.10) | copy-start | bytes 3076
  36.7 8.6 %copy-start = (bf16[64,8192]{1,0:T(8,128)(2,1)S(1)}, bf16[64,8192]{1,0:T(8,128)(2,1)}, u32[]{:S(2)}) copy-start(bf16[64,8192]{1,0:T(8,128)(2,1)} %param.7) | copy-start | bytes 3145732
  36.7 25.4 %all-to-all-start = ((bf16[32,2,8192]{2,1,0:T(2,128)(2,1)}), bf16[32,2,8192]{2,1,0:T(2,128)(2,1)S(1)}, u32[]{:S(2)}, u32[]{:S(2)}) async-start(bf16[32,2,8192]{2,1,0:T(2,128)(2,1)} %reshape.306), calls=%async_computation | async-start | bytes 2097152 | tf_op jit(solution)/shard_map/all_to_all | solution.py:34
  45.1 83.3 %all-gather.2.cloned.1.call-start = ((), (), s32[]{:S(2)}) async-start(), calls=%async_computation.3 | async-start | bytes 5242880 | tf_op jit(solution)/shard_map/all_gather | solution.py:54
  82.4 4.8 %slice-start = ((s8[8388608]{0:T(1024)(128)(4,1)}), s8[4194304]{0:T(1024)(128)(4,1)S(1)}, s32[]{:S(2)}) async-start(s8[8388608]{0:T(1024)(128)(4,1)} %bitcast.219), calls=%async_computation.4 | async-start | bytes 8388608
  86.3 3.1 %slice-start.1 = ((s8[8388608]{0:T(1024)(128)(4,1)}), s8[4194304]{0:T(1024)(128)(4,1)S(1)}, s32[]{:S(2)}) async-start(s8[8388608]{0:T(1024)(128)(4,1)} %bitcast.219), calls=%async_computation.5 | async-start | bytes 8388608
  86.9 15.1 %copy-start.1 = (bf16[8,64,8,128]{3,2,1,0:T(8,128)(2,1)}, bf16[8,64,8,128]{3,2,1,0:T(8,128)(2,1)S(1)}, u32[]{:S(2)}) copy-start(bf16[8,64,8,128]{3,2,1,0:T(8,128)(2,1)S(1)} %get-tuple-element.8) | copy-start | bytes 3145732
  87.2 21.1 %copy-start.2 = (bf16[8,64,8,128]{3,2,1,0:T(8,128)(2,1)}, bf16[8,64,8,128]{3,2,1,0:T(8,128)(2,1)S(1)}, u32[]{:S(2)}) copy-start(bf16[8,64,8,128]{3,2,1,0:T(8,128)(2,1)S(1)} %get-tuple-element.6) | copy-start | bytes 3145732
  112.5 15.9 %copy-start.6 = (bf16[16,64,4,64]{3,2,1,0:T(4,128)(2,1)S(1)}, bf16[16,64,4,64]{3,2,1,0:T(4,128)(2,1)}, u32[]{:S(2)}) copy-start(bf16[16,64,4,64]{3,2,1,0:T(4,128)(2,1)} %param.8) | copy-start | bytes 1572868
  132.9 18.0 %all-to-all-start.1 = ((bf16[16,4,64,128]{3,2,1,0:T(8,128)(2,1)}), bf16[16,4,64,128]{3,2,1,0:T(8,128)(2,1)S(1)}, u32[]{:S(2)}, u32[]{:S(2)}) async-start(bf16[16,4,64,128]{3,2,1,0:T(8,128)(2,1)} %copy.136), calls=%async_computation.1 | async-start | bytes 2097152 | tf_op jit(solution)/shard_map/all_to_all | solution.py:59
  152.6 25.6 %all-to-all-start.2 = ((bf16[4,16,64,128]{3,1,0,2:T(8,128)(2,1)}), bf16[4,16,64,128]{3,1,0,2:T(8,128)(2,1)}, u32[]{:S(2)}, u32[]{:S(2)}) async-start(bf16[4,16,64,128]{3,1,0,2:T(8,128)(2,1)} %copy.138), calls=%async_computation.2 | async-start | bytes 2097152 | tf_op jit(solution)/shard_map/all_to_all | solution.py:58
  182.5 2.7 %copy-start.3 = (f32[8192]{0:T(1024)S(1)}, f32[8192]{0:T(1024)}, u32[]{:S(2)}) copy-start(f32[8192]{0:T(1024)} %param.13) | copy-start | bytes 98308
  182.5 2.7 %copy-start.5 = (f32[64]{0:T(128)S(1)}, f32[64]{0:T(128)}, u32[]{:S(2)}) copy-start(f32[64]{0:T(128)} %param.12) | copy-start | bytes 772
Sparse Core Ops, SparseCore 0:
  82.6 45.7 all-gather.1
where the time goes:
time: 196 us; the launch traced here: 195 us
  matrix products  70.3 us (36%)
  local copies, waits for them, and re-layouts  56.1 us (29%)
  starting transfers between devices  27.7 us (14%)
  waiting for transfers between devices  23.9 us (12%)
  between operations  13.7 us (7%)
  other arithmetic  3.39 us (2%)
    dot_general x20, matrix products, local(): jnp.einsum('rcp,cpq->rcq', window, masked, preferred_element_type=jnp.flo...  66.9 us
    unnamed x25, local copies, waits for them, and re-layouts  21.7 us
    all_gather x1, waiting for transfers between devices, local(): all_rows = lax.all_gather(cycle_input, 'occ', axis=0, tiled=True)  13.9 us
    all_to_all x1, local copies, waits for them, and re-layouts, local(): lax.all_to_all(four_dim, 'vir', split_axis=3, concat_axis=2, tiled=True)  12.8 us
    reshape x2, local copies, waits for them, and re-layouts, local(): four_dim = amplitudes.reshape(outer_occ, NJ, NB_DEV, NA)  11.3 us
    all_to_all x1, starting transfers between devices, local(): lax.all_to_all(lax.all_to_all(cycle_part, 'occ', split_axis=0, concat_axi...  8.64 us
    all_to_all x1, starting transfers between devices, local(): lax.all_to_all(four_dim, 'vir', split_axis=3, concat_axis=2, tiled=True)  8.45 us
    all_to_all x1, waiting for transfers between devices, local(): lax.all_to_all(four_dim, 'vir', split_axis=3, concat_axis=2, tiled=True)  5.69 us
  transfers between devices with their start and end apart: 6, of which 4 were waited for; matrix products, arithmetic and copies ran while one was open for 57% of the time, Pallas kernels for 0%

commit v1 on v0

--- a/solution.py
+++ b/solution.py
@@ -31,7 +31,10 @@
     cols_dev = amplitudes.shape[1]
     outer_occ = rows_dev // NJ
     four_dim = amplitudes.reshape(outer_occ, NJ, NB_DEV, NA)
-    cycle_input = lax.all_to_all(four_dim, "vir", split_axis=3, concat_axis=2, tiled=True)
+    cycle_input = jnp.concatenate(
+        lax.all_to_all(jnp.stack(jnp.split(four_dim, lax.axis_size("vir"), axis=3)), "vir", 0, 0),
+        axis=2,
+    )
     tiles_dev = cols_dev // TILE
     padded = extended(amplitudes, (("vir", 1),), HT * TILE)
     own_tiles = lax.axis_index("vir") * tiles_dev + jnp.arange(tiles_dev, dtype=jnp.int32)

time: 196 us -> 177 us (0.903)
  local copies, waits for them, and re-layouts: 56.1 us -> 35.3 us
  matrix products: 70.3 us -> 74.8 us
  waiting for transfers between devices: 23.9 us -> 21.5 us
    all_to_all x1, local copies, waits for them, and re-layouts: 12.8 us -> 0.2 us  [local(): lax.all_to_all(jnp.stack(jnp.split(four_dim, lax.axis_size('vir'), axis=3...]
    reshape x2 -> x1, local copies, waits for them, and re-layouts: 11.3 us -> 1.83 us  [local(): four_dim = amplitudes.reshape(outer_occ, NJ, NB_DEV, NA)]
    dot_general x20, matrix products: 66.9 us -> 70.3 us  [local(): jnp.einsum('rcp,cpq->rcq', window, masked, preferred_element_type=jnp.flo...]
    all_gather x1, waiting for transfers between devices: 13.9 us -> 11.5 us  [local(): all_rows = lax.all_gather(cycle_input, 'occ', axis=0, tiled=True)]
    unnamed x25 -> x61, local copies, waits for them, and re-layouts: 21.7 us -> 21.9 us
  transfers between devices with their start and end apart: 6 -> 6, of which waited for: 4 -> 4; matrix products, arithmetic and copies ran while one was open for 57% -> 55% of each run, Pallas kernels for 0% -> 0%
where the time goes in v1:
time: 177 us; the launch traced here: 176 us
  matrix products  74.8 us (42%)
  local copies, waits for them, and re-layouts  35.3 us (20%)
  starting transfers between devices  27.7 us (16%)
  waiting for transfers between devices  21.5 us (12%)
  between operations  13.7 us (8%)
  other arithmetic  3.39 us (2%)
    dot_general x20, matrix products, local(): jnp.einsum('rcp,cpq->rcq', window, masked, preferred_element_type=jnp.flo...  70.3 us
    unnamed x61, local copies, waits for them, and re-layouts  21.9 us
    all_gather x1, waiting for transfers between devices, local(): all_rows = lax.all_gather(cycle_input, 'occ', axis=0, tiled=True)  11.5 us
    all_to_all x1, starting transfers between devices, local(): lax.all_to_all(lax.all_to_all(cycle_part, 'occ', split_axis=0, concat_axi...  8.63 us
    all_to_all x1, starting transfers between devices, local(): lax.all_to_all(jnp.stack(jnp.split(four_dim, lax.axis_size('vir'), axis=3...  8.31 us
    all_to_all x1, waiting for transfers between devices, local(): lax.all_to_all(jnp.stack(jnp.split(four_dim, lax.axis_size('vir'), axis=3...  5.57 us
    convert_element_type x2, local copies, waits for them, and re-layouts, local(): cycle_flat.astype(jnp.float32) + ladder  5.33 us
    ppermute x1, starting transfers between devices, extended(): lax.ppermute(lax.slice_in_dim(block, block.shape[dim] - width, None, axis...  4.92 us
  transfers between devices with their start and end apart: 6, of which 4 were waited for; matrix products, arithmetic and copies ran while one was open for 55% of the time, Pallas kernels for 0%

profile of v1, /device:TPU:1, one launch (start us, length us, event | category | flops | bytes accessed | tf_op | source)
XLA Modules:
  0.0 176.4 jit_solution(17974415051826759850)
XLA Ops:
  6.5 0.8 fusion.152
  7.3 4.9 %collective-permute-start = (bf16[64,256]{1,0:T(8,128)(2,1)S(1)}, bf16[64,256]{1,0:T(8,128)(2,1)S(1)}, u32[]{:S(2)}, u32[]{:S(2)}) collective-permute-start(bf16[64,256]{1,0:T(8,128)(2,1)S(1)} %get-tuple-element.11), channel_id=1, source_target_pairs={{0,1},{1,2},{2,3},{3,4},{4,5},{5,6},{6,7},{7,8},{8,9},{9,10},{10,1... | collective-permute-start | bytes 98312 | tf_op jit(solution)/shard_map/ppermute | solution.py:19
  12.2 1.9 %collective-permute-start.1 = (bf16[64,256]{1,0:T(8,128)(2,1)S(1)}, bf16[64,256]{1,0:T(8,128)(2,1)S(1)}, u32[]{:S(2)}, u32[]{:S(2)}) collective-permute-start(bf16[64,256]{1,0:T(8,128)(2,1)S(1)} %get-tuple-element.12), channel_id=1, source_target_pairs={{1,0},{2,1},{3,2},{4,3},{5,4},{6,5},{7,6},{8,7},{9,8},{10,9},{11,1... | collective-permute-start | bytes 98312 | tf_op jit(solution)/shard_map/ppermute | solution.py:22
  14.2 1.8 %reshape.300 = bf16[4,16,2,4096]{3,2,1,0:T(2,128)(2,1)S(1)} reshape(bf16[64,8192]{1,0:T(8,128)(2,1)} %param.7) | data formatting | bytes 2097152 | tf_op jit(solution)/shard_map/reshape | solution.py:33
  16.0 0.7 constant_dynamic-update-slice_fusion.31
  17.3 0.7 constant_dynamic-update-slice_fusion.29
  19.3 0.7 constant_dynamic-update-slice_fusion.26
  22.6 0.7 constant_dynamic-update-slice_fusion.21
  24.5 0.7 constant_dynamic-update-slice_fusion.18
  26.5 0.7 constant_dynamic-update-slice_fusion.15
  27.8 0.7 constant_dynamic-update-slice_fusion.13
  29.7 0.7 constant_dynamic-update-slice_fusion.10
  31.7 0.7 constant_dynamic-update-slice_fusion.7
  36.9 8.3 %all-to-all-start = ((bf16[32,4,16,2,128]{4,3,2,1,0:T(2,128)(2,1)}), bf16[32,4,16,2,128]{4,3,2,1,0:T(2,128)(2,1)S(1)}, u32[]{:S(2)}, u32[]{:S(2)}) async-start(bf16[32,4,16,2,128]{4,3,2,1,0:T(2,128)(2,1)} %constant_dynamic-update-slice_fusion), calls=%async_computation | async-start | bytes 2097152 | tf_op jit(solution)/shard_map/all_to_all | solution.py:35
  45.4 3.7 %fusion.12 = f32[64,128,64]{1,2,0:T(8,128)} fusion(pred[64]{0:T(512)(128)(4,1)S(1)} %get-tuple-element.23, bf16[64,4,128,128]{3,2,1,0:T(8,128)(2,1)} %param.9, bf16[64,8192]{1,0:T(8,128)(2,1)S(1)} %copy-done), kind=kOutput, calls=%fused_computation.23 | convolution fusion | flops 135266304 | bytes 5242944 | tf_op jit(solution)/shard_map/rcp,cpq->rcq/dot_general | solution.py:53
  49.1 3.7 %fusion.17 = f32[64,128,64]{1,2,0:T(8,128)} fusion(pred[64]{0:T(512)(128)(4,1)S(1)} %get-tuple-element.15, bf16[64,4,128,128]{3,2,1,0:T(8,128)(2,1)} %param.9, bf16[64,8192]{1,0:T(8,128)(2,1)S(1)} %copy-done), kind=kOutput, calls=%fused_computation.33 | convolution fusion | flops 135266304 | bytes 5242944 | tf_op jit(solution)/shard_map/rcp,cpq->rcq/dot_general | solution.py:53
  52.8 3.7 %fusion.23 = f32[64,128,64]{1,2,0:T(8,128)} fusion(pred[64]{0:T(512)(128)(4,1)S(1)} %get-tuple-element.19, bf16[64,4,128,128]{3,2,1,0:T(8,128)(2,1)} %param.9, bf16[64,8192]{1,0:T(8,128)(2,1)S(1)} %copy-done), kind=kOutput, calls=%fused_computation.48 | convolution fusion | flops 135266304 | bytes 5242944 | tf_op jit(solution)/shard_map/rcp,cpq->rcq/dot_general | solution.py:53
  56.5 5.6 %all-to-all-done = bf16[32,4,16,2,128]{4,3,2,1,0:T(2,128)(2,1)S(1)} async-done(((bf16[32,4,16,2,128]{4,3,2,1,0:T(2,128)(2,1)}), bf16[32,4,16,2,128]{4,3,2,1,0:T(2,128)(2,1)S(1)}, u32[]{:S(2)}, u32[]{:S(2)}) %all-to-all-start) | async-done | bytes 1048608 | tf_op jit(solution)/shard_map/all_to_all | solution.py:35
  62.3 1.2 copy.194
  63.6 3.8 %fusion.7 = f32[64,128,64]{1,2,0:T(8,128)} fusion(pred[64]{0:T(512)(128)(4,1)S(1)} %get-tuple-element.27, bf16[64,4,128,128]{3,2,1,0:T(8,128)(2,1)} %param.9, bf16[64,8192]{1,0:T(8,128)(2,1)S(1)} %copy-done), kind=kOutput, calls=%fused_computation.13 | convolution fusion | flops 135266304 | bytes 5242944 | tf_op jit(solution)/shard_map/rcp,cpq->rcq/dot_general | solution.py:53
  67.4 1.0 copy.195
  69.4 5.7 %fusion.13 = f32[64,128,64]{1,2,0:T(8,128)} fusion(pred[64]{0:T(512)(128)(4,1)S(1)} %get-tuple-element.24, bf16[64,4,128,128]{3,2,1,0:T(8,128)(2,1)} %param.9, bf16[8,64,8,128]{3,2,1,0:T(8,128)(2,1)S(1)} %get-tuple-element.7), kind=kOutput, calls=%fused_computation.24 | convolution fusion | flops 135266304 | bytes 5242944 | tf_op jit(solution)/shard_map/rcp,cpq->rcq/dot_general | solution.py:53
  75.1 2.1 %fusion.18 = f32[64,128,64]{1,2,0:T(8,128)} fusion(pred[64]{0:T(512)(128)(4,1)S(1)} %get-tuple-element.16, bf16[64,4,128,128]{3,2,1,0:T(8,128)(2,1)S(1)} %bitcast.347, bf16[8,64,8,128]{3,2,1,0:T(8,128)(2,1)S(1)} %get-tuple-element.7), kind=kOutput, calls=%fused_computation.34 | convolution fusion | flops 135266304 | bytes 5243392 | tf_op jit(solution)/shard_map/rcp,cpq->rcq/dot_general | solution.py:53
  77.2 2.1 %fusion.14 = f32[64,128,64]{1,2,0:T(8,128)} fusion(pred[64]{0:T(512)(128)(4,1)S(1)} %get-tuple-element.25, bf16[64,4,128,128]{3,2,1,0:T(8,128)(2,1)S(1)} %bitcast.347, bf16[8,64,8,128]{3,2,1,0:T(8,128)(2,1)S(1)} %get-tuple-element.8), kind=kOutput, calls=%fused_computation.25 | convolution fusion | flops 135266304 | bytes 5243392 | tf_op jit(solution)/shard_map/rcp,cpq->rcq/dot_general | solution.py:53
  79.3 2.1 %fusion.19 = f32[64,128,64]{1,2,0:T(8,128)} fusion(pred[64]{0:T(512)(128)(4,1)S(1)} %get-tuple-element.17, bf16[64,4,128,128]{3,2,1,0:T(8,128)(2,1)S(1)} %bitcast.347, bf16[8,64,8,128]{3,2,1,0:T(8,128)(2,1)S(1)} %get-tuple-element.8), kind=kOutput, calls=%fused_computation.35 | convolution fusion | flops 135266304 | bytes 5243392 | tf_op jit(solution)/shard_map/rcp,cpq->rcq/dot_general | solution.py:53
  81.4 2.1 %fusion.24 = f32[64,128,64]{1,2,0:T(8,128)} fusion(pred[64]{0:T(512)(128)(4,1)S(1)} %get-tuple-element.20, bf16[64,4,128,128]{3,2,1,0:T(8,128)(2,1)S(1)} %bitcast.347, bf16[8,64,8,128]{3,2,1,0:T(8,128)(2,1)S(1)} %get-tuple-element.7), kind=kOutput, calls=%fused_computation.49 | convolution fusion | flops 135266304 | bytes 5243392 | tf_op jit(solution)/shard_map/rcp,cpq->rcq/dot_general | solution.py:53
  83.5 2.1 %fusion.8 = f32[64,128,64]{1,2,0:T(8,128)} fusion(pred[64]{0:T(512)(128)(4,1)S(1)} %get-tuple-element.28, bf16[64,4,128,128]{3,2,1,0:T(8,128)(2,1)S(1)} %bitcast.347, bf16[8,64,8,128]{3,2,1,0:T(8,128)(2,1)S(1)} %get-tuple-element.7), kind=kOutput, calls=%fused_computation.14 | convolution fusion | flops 135266304 | bytes 5243392 | tf_op jit(solution)/shard_map/rcp,cpq->rcq/dot_general | solution.py:53
  85.6 2.1 %fusion.9 = f32[64,128,64]{1,2,0:T(8,128)} fusion(pred[64]{0:T(512)(128)(4,1)S(1)} %get-tuple-element.29, bf16[64,4,128,128]{3,2,1,0:T(8,128)(2,1)S(1)} %bitcast.347, bf16[8,64,8,128]{3,2,1,0:T(8,128)(2,1)S(1)} %get-tuple-element.8), kind=kOutput, calls=%fused_computation.15 | convolution fusion | flops 135266304 | bytes 5243392 | tf_op jit(solution)/shard_map/rcp,cpq->rcq/dot_general | solution.py:53
  87.7 2.1 %fusion.11 = f32[64,128,64]{1,2,0:T(8,128)} fusion(pred[64]{0:T(512)(128)(4,1)S(1)} %get-tuple-element.21, bf16[64,4,128,128]{3,2,1,0:T(8,128)(2,1)S(1)} %bitcast.347, bf16[8,64,8,128]{3,2,1,0:T(8,128)(2,1)S(1)} %get-tuple-element.6), kind=kOutput, calls=%fused_computation.22 | convolution fusion | flops 135266304 | bytes 5243392 | tf_op jit(solution)/shard_map/rcp,cpq->rcq/dot_general | solution.py:53
  89.8 2.1 %fusion.16 = f32[64,128,64]{1,2,0:T(8,128)} fusion(pred[64]{0:T(512)(128)(4,1)S(1)} %get-tuple-element.14, bf16[64,4,128,128]{3,2,1,0:T(8,128)(2,1)S(1)} %bitcast.347, bf16[8,64,8,128]{3,2,1,0:T(8,128)(2,1)S(1)} %get-tuple-element.6), kind=kOutput, calls=%fused_computation.32 | convolution fusion | flops 135266304 | bytes 5243392 | tf_op jit(solution)/shard_map/rcp,cpq->rcq/dot_general | solution.py:53
  91.8 2.1 %fusion.22 = f32[64,128,64]{1,2,0:T(8,128)} fusion(pred[64]{0:T(512)(128)(4,1)S(1)} %get-tuple-element.18, bf16[64,4,128,128]{3,2,1,0:T(8,128)(2,1)S(1)} %bitcast.347, bf16[8,64,8,128]{3,2,1,0:T(8,128)(2,1)S(1)} %get-tuple-element.6), kind=kOutput, calls=%fused_computation.47 | convolution fusion | flops 135266304 | bytes 5243392 | tf_op jit(solution)/shard_map/rcp,cpq->rcq/dot_general | solution.py:53
  93.9 2.1 %fusion.21 = f32[64,128,64]{1,2,0:T(8,128)} fusion(pred[64]{0:T(512)(128)(4,1)S(1)} %get-tuple-element.22, bf16[64,4,128,128]{3,2,1,0:T(8,128)(2,1)S(1)} %bitcast.347, bf16[8,64,8,128]{3,2,1,0:T(8,128)(2,1)S(1)} %get-tuple-element.5), kind=kOutput, calls=%fused_computation.46 | convolution fusion | flops 135266304 | bytes 5243392 | tf_op jit(solution)/shard_map/rcp,cpq->rcq/dot_general | solution.py:53
  96.0 2.1 %fusion.5 = f32[64,128,64]{1,2,0:T(8,128)} fusion(pred[64]{0:T(512)(128)(4,1)S(1)} %get-tuple-element.30, bf16[64,4,128,128]{3,2,1,0:T(8,128)(2,1)S(1)} %bitcast.347, bf16[8,64,8,128]{3,2,1,0:T(8,128)(2,1)S(1)} %get-tuple-element.5), kind=kOutput, calls=%fused_computation.11 | convolution fusion | flops 135266304 | bytes 5243392 | tf_op jit(solution)/shard_map/rcp,cpq->rcq/dot_general | solution.py:53
  98.1 11.5 %all-gather.2.cloned.1.call-done = bf16[16,16,64,128]{3,2,1,0:T(8,128)(2,1)} async-done(((bf16[4,16,64,128]{3,2,1,0:T(8,128)(2,1)}), bf16[16,16,64,128]{3,2,1,0:T(8,128)(2,1)}) %all-gather.2.cloned.1.call-update) | async-done | bytes 4194320 | tf_op jit(solution)/shard_map/all_gather | solution.py:57
  109.5 4.5 %fusion.48 = bf16[16,4,64,128]{3,2,1,0:T(8,128)(2,1)} fusion(bf16[16,16,64,128]{3,2,1,0:T(8,128)(2,1)} %all-gather.2.cloned.1.call-done, bf16[16,64,4,64]{1,3,0,2:T(8,128)(2,1)S(1)} %copy.195), kind=kOutput, calls=%fused_computation.72 | convolution fusion | flops 1074266112 | bytes 5767168 | tf_op jit(solution)/shard_map/ijba,jbkc->ikca/dot_general | solution.py:58
  114.0 3.9 %all-to-all-start.1 = ((bf16[16,4,64,128]{3,2,1,0:T(8,128)(2,1)}), bf16[16,4,64,128]{3,2,1,0:T(8,128)(2,1)S(1)}, u32[]{:S(2)}, u32[]{:S(2)}) async-start(bf16[16,4,64,128]{3,2,1,0:T(8,128)(2,1)} %fusion.48), calls=%async_computation.1 | async-start | bytes 2097152 | tf_op jit(solution)/shard_map/all_to_all | solution.py:62
  117.9 3.8 %fusion.6 = f32[64,128,64]{1,2,0:T(8,128)} fusion(pred[64]{0:T(512)(128)(4,1)S(1)} %get-tuple-element.26, bf16[64,4,128,128]{3,2,1,0:T(8,128)(2,1)} %param.9, bf16[8,64,8,128]{3,2,1,0:T(8,128)(2,1)S(1)} %copy-done.6), kind=kOutput, calls=%fused_computation.12 | convolution fusion | flops 135266304 | bytes 5242944 | tf_op jit(solution)/shard_map/rcp,cpq->rcq/dot_general | solution.py:53
  121.7 3.7 %fusion.10 = f32[64,128,64]{1,2,0:T(8,128)} fusion(pred[64]{0:T(512)(128)(4,1)S(1)} %get-tuple-element.32, bf16[64,4,128,128]{3,2,1,0:T(8,128)(2,1)} %param.9, bf16[8,64,8,128]{3,2,1,0:T(8,128)(2,1)S(1)} %copy-done.4), kind=kOutput, calls=%fused_computation.21 | convolution fusion | flops 135266304 | bytes 5242944 | tf_op jit(solution)/shard_map/rcp,cpq->rcq/dot_general | solution.py:53
  125.4 3.6 %fusion.15 = f32[64,128,64]{1,2,0:T(8,128)} fusion(pred[64]{0:T(512)(128)(4,1)S(1)} %get-tuple-element.31, bf16[64,4,128,128]{3,2,1,0:T(8,128)(2,1)} %param.9, bf16[8,64,8,128]{3,2,1,0:T(8,128)(2,1)S(1)} %copy-done.4), kind=kOutput, calls=%fused_computation.31 | convolution fusion | flops 135266304 | bytes 5242944 | tf_op jit(solution)/shard_map/rcp,cpq->rcq/dot_general | solution.py:53
  129.0 3.1 %all-to-all-done.1 = bf16[16,4,64,128]{3,2,1,0:T(8,128)(2,1)S(1)} async-done(((bf16[16,4,64,128]{3,2,1,0:T(8,128)(2,1)}), bf16[16,4,64,128]{3,2,1,0:T(8,128)(2,1)S(1)}, u32[]{:S(2)}, u32[]{:S(2)}) %all-to-all-start.1) | async-done | bytes 1048608 | tf_op jit(solution)/shard_map/all_to_all | solution.py:62
  132.2 1.6 copy.197
  133.9 8.6 %all-to-all-start.2 = ((bf16[4,16,64,128]{3,1,0,2:T(8,128)(2,1)}), bf16[4,16,64,128]{3,1,0,2:T(8,128)(2,1)}, u32[]{:S(2)}, u32[]{:S(2)}) async-start(bf16[4,16,64,128]{3,1,0,2:T(8,128)(2,1)} %copy.197), calls=%async_computation.2 | async-start | bytes 2097152 | tf_op jit(solution)/shard_map/all_to_all | solution.py:61
  142.5 15.6 %fusion.20 = f32[64,8,8,128]{3,2,1,0:T(8,128)S(1)} fusion(f32[64,128,64]{1,2,0:T(8,128)} %fusion.9, f32[64,128,64]{1,2,0:T(8,128)} %fusion.14, f32[64,128,64]{1,2,0:T(8,128)} %fusion.19, f32[64,128,64]{1,2,0:T(8,128)} %fusion.8, f32[64,128,64]{1,2,0:T(8,128)} %fusion.13, f32[64,128,64]{1,2,0:T(8,128)} %fusion.24, f32[64,128,64]{1,2,0:T(8,128)} %fusion.18, ...), kind=kOutput, calls=%fused_computation.38 | convolution fusion | flops 145227776 | bytes 45088832 | tf_op jit(solution)/shard_map/rcp,cpq->rcq/dot_general | solution.py:53
  158.1 1.4 all-to-all-done.2
  159.5 1.4 copy.198
  161.2 2.6 %copy.199 = f32[4,16,2,32,128]{4,3,2,1,0:T(8,128)} copy(f32[4,16,2,32,128]{4,1,2,3,0:T(8,128)S(1)} %convert_bitcast_fusion) | data formatting | bytes 4194304 | tf_op jit(solution)/shard_map/convert_element_type | solution.py:71
  163.7 2.7 %reshape.309 = f32[64,8192]{1,0:T(8,128)} reshape(f32[4,16,2,32,128]{4,3,2,1,0:T(8,128)} %copy.199) | data formatting | bytes 4194304 | tf_op jit(solution)/shard_map/convert_element_type | solution.py:71
  166.5 3.1 %fusion.4 = bf16[64,8192]{1,0:T(8,128)(2,1)} fusion(f32[64,8192]{1,0:T(8,128)} %reshape.309, f32[64,8,8,128]{3,2,1,0:T(8,128)S(1)} %fusion.20, bf16[64,8192]{1,0:T(8,128)(2,1)S(1)} %copy-done, f32[8192]{0:T(1024)S(1)} %copy-done.7, f32[64]{0:T(128)S(1)} %copy-done.9), kind=kLoop, calls=%fused_computation.5 | loop fusion | flops 3145728 | bytes 6324480 | tf_op jit(solution)/shard_map/convert_element_type | solution.py:73
  (68 shorter events, 16.6 us)
Async XLA Ops:
  7.3 61.1 %collective-permute-start = (bf16[64,256]{1,0:T(8,128)(2,1)S(1)}, bf16[64,256]{1,0:T(8,128)(2,1)S(1)}, u32[]{:S(2)}, u32[]{:S(2)}) collective-permute-start(bf16[64,256]{1,0:T(8,128)(2,1)S(1)} %get-tuple-element.11), channel_id=1, source_target_pairs={{0,1},{1,2},{2,3},{3,4},{4,5},{5,6},{6,7},{7,8},{8,9},{9,10},{10,1... | collective-permute-start | bytes 98312 | tf_op jit(solution)/shard_map/ppermute | solution.py:19
  12.2 56.3 %collective-permute-start.1 = (bf16[64,256]{1,0:T(8,128)(2,1)S(1)}, bf16[64,256]{1,0:T(8,128)(2,1)S(1)}, u32[]{:S(2)}, u32[]{:S(2)}) collective-permute-start(bf16[64,256]{1,0:T(8,128)(2,1)S(1)} %get-tuple-element.12), channel_id=1, source_target_pairs={{1,0},{2,1},{3,2},{4,3},{5,4},{6,5},{7,6},{8,7},{9,8},{10,9},{11,1... | collective-permute-start | bytes 98312 | tf_op jit(solution)/shard_map/ppermute | solution.py:22
  16.0 29.2 %copy-start.10 = (s32[64]{0:T(128)S(1)}, s32[64]{0:T(128)}, u32[]{:S(2)}) copy-start(s32[64]{0:T(128)} %param.11) | copy-start | bytes 772
  16.0 29.3 %copy-start.8 = (s32[64,4]{0,1:T(4,128)S(1)}, s32[64,4]{0,1:T(4,128)}, u32[]{:S(2)}) copy-start(s32[64,4]{0,1:T(4,128)} %param.10) | copy-start | bytes 3076
  16.7 28.7 %copy-start = (bf16[64,8192]{1,0:T(8,128)(2,1)S(1)}, bf16[64,8192]{1,0:T(8,128)(2,1)}, u32[]{:S(2)}) copy-start(bf16[64,8192]{1,0:T(8,128)(2,1)} %param.7) | copy-start | bytes 3145732
  36.9 25.2 %all-to-all-start = ((bf16[32,4,16,2,128]{4,3,2,1,0:T(2,128)(2,1)}), bf16[32,4,16,2,128]{4,3,2,1,0:T(2,128)(2,1)S(1)}, u32[]{:S(2)}, u32[]{:S(2)}) async-start(bf16[32,4,16,2,128]{4,3,2,1,0:T(2,128)(2,1)} %constant_dynamic-update-slice_fusion), calls=%async_computation | async-start | bytes 2097152 | tf_op jit(solution)/shard_map/all_to_all | solution.py:35
  45.2 64.3 %all-gather.2.cloned.1.call-start = ((), (), s32[]{:S(2)}) async-start(), calls=%async_computation.3 | async-start | bytes 5242880 | tf_op jit(solution)/shard_map/all_gather | solution.py:57
  63.6 3.8 %copy-start.2 = (bf16[16,64,4,64]{3,2,1,0:T(4,128)(2,1)S(1)}, bf16[16,64,4,64]{3,2,1,0:T(4,128)(2,1)}, u32[]{:S(2)}) copy-start(bf16[16,64,4,64]{3,2,1,0:T(4,128)(2,1)} %param.8) | copy-start | bytes 1572868
  68.4 6.7 %slice-start = ((s8[8388608]{0:T(1024)(128)(4,1)}), s8[4194304]{0:T(1024)(128)(4,1)S(1)}, s32[]{:S(2)}) async-start(s8[8388608]{0:T(1024)(128)(4,1)} %bitcast.346), calls=%async_computation.4 | async-start | bytes 8388608
  69.0 16.6 %copy-start.1 = (bf16[8,64,8,128]{3,2,1,0:T(8,128)(2,1)}, bf16[8,64,8,128]{3,2,1,0:T(8,128)(2,1)S(1)}, u32[]{:S(2)}) copy-start(bf16[8,64,8,128]{3,2,1,0:T(8,128)(2,1)S(1)} %get-tuple-element.8) | copy-start | bytes 3145732
  69.0 6.1 %slice-start.1 = ((s8[8388608]{0:T(1024)(128)(4,1)}), s8[4194304]{0:T(1024)(128)(4,1)S(1)}, s32[]{:S(2)}) async-start(s8[8388608]{0:T(1024)(128)(4,1)} %bitcast.346), calls=%async_computation.5 | async-start | bytes 8388608
  69.4 22.5 %copy-start.5 = (bf16[8,64,8,128]{3,2,1,0:T(8,128)(2,1)}, bf16[8,64,8,128]{3,2,1,0:T(8,128)(2,1)S(1)}, u32[]{:S(2)}) copy-start(bf16[8,64,8,128]{3,2,1,0:T(8,128)(2,1)S(1)} %get-tuple-element.6) | copy-start | bytes 3145732
  69.4 26.6 %copy-start.3 = (bf16[8,64,8,128]{3,2,1,0:T(8,128)(2,1)}, bf16[8,64,8,128]{3,2,1,0:T(8,128)(2,1)S(1)}, u32[]{:S(2)}) copy-start(bf16[8,64,8,128]{3,2,1,0:T(8,128)(2,1)S(1)} %get-tuple-element.5) | copy-start | bytes 3145732
  114.0 3.9 %copy-start.6 = (bf16[8,64,8,128]{3,2,1,0:T(8,128)(2,1)S(1)}, bf16[8,64,8,128]{3,2,1,0:T(8,128)(2,1)}, u32[]{:S(2)}) copy-start(bf16[8,64,8,128]{3,2,1,0:T(8,128)(2,1)} %copy-done.5) | copy-start | bytes 3145732
  114.0 18.1 %all-to-all-start.1 = ((bf16[16,4,64,128]{3,2,1,0:T(8,128)(2,1)}), bf16[16,4,64,128]{3,2,1,0:T(8,128)(2,1)S(1)}, u32[]{:S(2)}, u32[]{:S(2)}) async-start(bf16[16,4,64,128]{3,2,1,0:T(8,128)(2,1)} %fusion.48), calls=%async_computation.1 | async-start | bytes 2097152 | tf_op jit(solution)/shard_map/all_to_all | solution.py:62
  117.9 3.8 %copy-start.4 = (bf16[8,64,8,128]{3,2,1,0:T(8,128)(2,1)S(1)}, bf16[8,64,8,128]{3,2,1,0:T(8,128)(2,1)}, u32[]{:S(2)}) copy-start(bf16[8,64,8,128]{3,2,1,0:T(8,128)(2,1)} %copy-done.3) | copy-start | bytes 3145732
  133.9 25.6 %all-to-all-start.2 = ((bf16[4,16,64,128]{3,1,0,2:T(8,128)(2,1)}), bf16[4,16,64,128]{3,1,0,2:T(8,128)(2,1)}, u32[]{:S(2)}, u32[]{:S(2)}) async-start(bf16[4,16,64,128]{3,1,0,2:T(8,128)(2,1)} %copy.197), calls=%async_computation.2 | async-start | bytes 2097152 | tf_op jit(solution)/shard_map/all_to_all | solution.py:61
  163.7 2.8 %copy-start.7 = (f32[8192]{0:T(1024)S(1)}, f32[8192]{0:T(1024)}, u32[]{:S(2)}) copy-start(f32[8192]{0:T(1024)} %param.13) | copy-start | bytes 98308
  163.7 2.8 %copy-start.9 = (f32[64]{0:T(128)S(1)}, f32[64]{0:T(128)}, u32[]{:S(2)}) copy-start(f32[64]{0:T(128)} %param.12) | copy-start | bytes 772
Sparse Core Ops, SparseCore 0:
  63.7 45.7 all-gather.1
